TPU v7x, 32 devices: a whole 2x2x4 slice. The times are simulated.
32 devices in a mesh: gx: 4 (over x, core), gy: 8 (over z, y).
Axes of the slice: x: 2, y: 2, z: 4, core: 2. Of those that a mesh axis runs over, the one named last changes fastest.
Arguments:
- text_feats: bfloat16 [16384, 1152], P(('gx', 'gy')), may hold values from -0.75 to 0.75
- proj: float32 [1152, 1152], P(('gx', 'gy')), may hold values from -0.1875 to 0.1875
- first_moment: float32 [1152, 1152], P(('gx', 'gy')), may hold values from -12 to 12
- second_moment: float32 [1152, 1152], P(('gx', 'gy')), may hold values from 0.1 to 10
- owners: int32 [1024, 5], P(('gx', 'gy')), may hold values from 0 to 31, all different within a row; in each aligned block of 32 rows (0 to 31, 32 to 63, ...) at most 6 rows name the same one
- blocks: int32 [1024, 5], P(('gx', 'gy')), may hold values from 0 to 11
- positives: int32 [16384], P(('gx', 'gy')), may hold values from 0 to 3071
- bank: bfloat16 [98304, 1152], P(('gx', 'gy')), may hold values from -0.1875 to 0.1875
Outputs:
- text_grad: bfloat16 [16384, 1152], P(('gx', 'gy'))
- new_proj: float32 [1152, 1152], P(('gx', 'gy'))
- new_first: float32 [1152, 1152], P(('gx', 'gy'))
- new_second: float32 [1152, 1152], P(('gx', 'gy'))
Inputs may be any that keep to these rules, and one draw needn't show every extreme that they name: `owners`: each row names 5 different owner devices, counted in the order gx then gy. Among the text blocks of one device no owner is named more than 6 times, and in some devices' blocks an owner is named exactly 6 times. `positives`: each text row's positive lies in its own device's bank, counted from that device's first bank row.
All inputs are finite; a program needn't handle non-finite values.
Results may differ from a plain program's by a relative error of at most 0.0095.
Values may be sent and summed in bfloat16 or wider, within the bound.
No kernel may reach another device: no remote copies, remote signals or barrier semaphores. Data moves between devices by JAX's collectives and lax.ppermute only.
A program may use at most 128 MiB of HBM per device.

v0:
```python
import functools

import jax
import jax.numpy as jnp
from jax import lax
from jax.experimental import pallas as pl
from jax.experimental.pallas import tpu as pltpu
from jax.sharding import Mesh, PartitionSpec as P


BROWS = 256
TILE_SLOTS = 8

logit_scale = 20.0
logit_bias = -3.0
norm_eps = 1e-06
beta_one = 0.9
beta_two = 0.999
learn_rate = 0.001
decay_rate = 0.1
adam_eps = 1e-08
adam_step = 100.0

ALL = ("x", "c", "zh", "zl", "y")
PLANE = ("x", "c", "y")
COLUMN = ("zh", "zl")
SWAP = [(0, 1), (1, 0)]
bf16 = jnp.bfloat16
f32 = jnp.float32


def answer_kernel(groups, slots, tb, banks, row_chunk, tags_ref, *refs):
    x_hbm, (w_hbm, bank_hbm), out_hbm = refs[:groups], refs[groups : groups + 2], refs[groups + 2 : 2 * groups + 2]
    (x_ref, w_ref, bank_ref, unit_ref, order_ref, count_ref, tile_bank, tile_first, tile_last, x_sem, w_sem, bank_sem, out_sem) = refs[2 * groups + 2 :]
    rows = slots * tb
    w_copy = pltpu.make_async_copy(w_hbm, w_ref, w_sem)
    bank_copy = pltpu.make_async_copy(bank_hbm, bank_ref, bank_sem)
    x_copies = [
        pltpu.make_async_copy(x_hbm[g], x_ref.at[pl.ds(g * rows, rows), :], x_sem.at[g]) for g in range(groups)
    ]
    w_copy.start()
    for copy in x_copies:
        copy.start()
    bank_copy.start()
    total = groups * slots

    for b in range(banks):
        count_ref[b] = 0

    def count(s, carry):
        b = tags_ref[s]
        count_ref[b] = count_ref[b] + 1
        return carry

    lax.fori_loop(0, total, count, 0)

    def lay(b, carry):
        first, tiles = carry
        n = count_ref[b]
        last = first + n - 1

        def tile(i, carry):
            tile_bank[tiles + i] = b
            tile_first[tiles + i] = first + i * TILE_SLOTS
            tile_last[tiles + i] = last
            return carry

        n_tiles = lax.div(n + TILE_SLOTS - 1, TILE_SLOTS)
        lax.fori_loop(0, n_tiles, tile, 0)
        count_ref[b] = first
        return first + n, tiles + n_tiles

    _, n_tiles = lax.fori_loop(0, banks, lay, (0, 0))

    def place(s, carry):
        b = tags_ref[s]
        at = count_ref[b]
        order_ref[at] = s
        count_ref[b] = at + 1
        return carry

    lax.fori_loop(0, total, place, 0)

    def project(i, carry):
        part = pl.ds(pl.multiple_of(i * row_chunk, row_chunk), row_chunk)
        projected = jnp.dot(x_ref[part, :], w_ref[...], preferred_element_type=f32)
        radius = jnp.sqrt(jnp.sum(projected * projected, axis=-1, keepdims=True) + norm_eps)
        unit_ref[part, :] = (projected * (1.0 / radius)).astype(bf16)
        return carry

    w_copy.wait()
    for copy in x_copies:
        copy.wait()
    lax.fori_loop(0, groups * rows // row_chunk, project, 0)
    bank_copy.wait()

    def answer_tile(t, carry):
        b = tile_bank[t]
        first = tile_first[t]
        last = tile_last[t]
        at = []
        for i in range(TILE_SLOTS):
            at.append(pl.multiple_of(order_ref[jnp.minimum(first + i, last)] * tb, tb))
        queries = jnp.concatenate([unit_ref[pl.ds(a, tb), :] for a in at], axis=0)
        keys = bank_ref[pl.ds(pl.multiple_of(b * BROWS, BROWS), BROWS), :]
        scores = lax.dot_general(queries, keys, (((1,), (1,)), ((), ())), preferred_element_type=f32)
        coef = jax.nn.sigmoid(logit_scale * scores + logit_bias).astype(bf16)
        grad = logit_scale * jnp.dot(coef, keys, preferred_element_type=f32)
        grad = grad.astype(bf16)
        for i, a in enumerate(at):
            x_ref[pl.ds(a, tb), :] = grad[i * tb : (i + 1) * tb, :]
        return carry

    lax.fori_loop(0, n_tiles, answer_tile, 0)
    out_copies = [
        pltpu.make_async_copy(x_ref.at[pl.ds(g * rows, rows), :], out_hbm[g], out_sem.at[g]) for g in range(groups)
    ]
    for copy in out_copies:
        copy.start()
    for copy in out_copies:
        copy.wait()


def answer(xs, tags, weight_half, bank, tb):
    groups = len(xs)
    rows, width = xs[0].shape
    slots = rows // tb
    banks = bank.shape[0] // BROWS
    most_tiles = groups * slots // TILE_SLOTS + banks + 1
    row_chunk = 128 if rows % 128 == 0 else tb
    hbm = pl.BlockSpec(memory_space=pltpu.HBM)
    return pl.pallas_call(
        functools.partial(answer_kernel, groups, slots, tb, banks, row_chunk),
        out_shape=[jax.ShapeDtypeStruct((rows, width), bf16)] * groups,
        in_specs=[pl.BlockSpec(memory_space=pltpu.SMEM)] + [hbm] * (groups + 2),
        out_specs=[hbm] * groups,
        scratch_shapes=[
            pltpu.VMEM((groups * rows, width), bf16),
            pltpu.VMEM(weight_half.shape, bf16),
            pltpu.VMEM(bank.shape, bf16),
            pltpu.VMEM((groups * rows, width), bf16),
            pltpu.SMEM((groups * slots,), jnp.int32),
            pltpu.SMEM((banks,), jnp.int32),
            pltpu.SMEM((most_tiles,), jnp.int32),
            pltpu.SMEM((most_tiles,), jnp.int32),
            pltpu.SMEM((most_tiles,), jnp.int32),
            pltpu.SemaphoreType.DMA((groups,)),
            pltpu.SemaphoreType.DMA,
            pltpu.SemaphoreType.DMA,
            pltpu.SemaphoreType.DMA((groups,)),
        ],
        compiler_params=pltpu.CompilerParams(vmem_limit_bytes=60 << 20),
        cost_estimate=pl.CostEstimate(
            flops=groups * (2 * rows * width * width + 8 * rows * width * BROWS),
            bytes_accessed=groups * 4 * rows * width + 2 * width * width + 2 * bank.size,
            transcendentals=groups * rows * BROWS,
        ),
        name="answer",
    )(tags, *xs, weight_half, bank)


def finish_kernel(n_x, n_z, n_y, piece, c_ref, base_ref, high_ref, unit_ref, radius_ref, text_ref, p_ref, send_ref, keep_ref, g_ref):
    at = pl.program_id(0)
    embed = base_ref[...] + high_ref[...].astype(f32)
    unit = unit_ref[...]
    radial = jnp.sum(unit * embed, axis=-1, keepdims=True)
    p = ((embed - unit * radial) / radius_ref[...]).astype(bf16)
    p_ref[...] = p
    grad = jnp.dot(text_ref[...], p, preferred_element_type=f32)

    @pl.when(at == 0)
    def _():
        g_ref[...] = grad

    @pl.when(at > 0)
    def _():
        g_ref[...] += grad

    for core in range(2):

        @pl.when((at == pl.num_programs(0) - 1) & (c_ref[0] == core))
        def _():
            for x in range(n_x):
                for y in range(n_y):
                    for z in range(n_z):
                        mine = (((x * 2 + core) * n_z + z) * n_y + y) * piece
                        other = (((x * 2 + 1 - core) * n_z + z) * n_y + y) * piece
                        keep_ref[x * n_y + y, z, :piece, :] = g_ref[mine : mine + piece, :]
                        send_ref[x * n_y + y, z, :piece, :] = g_ref[other : other + piece, :].astype(bf16)


def finish(c, base, from_high, unit_rows, radius, text_t, n_x, n_z, n_y):
    rows, width = base.shape
    depth = text_t.shape[0]
    piece = depth // (n_x * 2 * n_z * n_y)
    tall = piece + -piece % 8
    steps = 2
    block = rows // steps
    by_row = pl.BlockSpec((block, width), lambda i: (i, 0))
    whole = pl.BlockSpec((n_x * n_y, n_z, tall, width), lambda i: (0, 0, 0, 0))
    return pl.pallas_call(
        functools.partial(finish_kernel, n_x, n_z, n_y, piece),
        grid=(steps,),
        out_shape=[
            jax.ShapeDtypeStruct((rows, width), bf16),
            jax.ShapeDtypeStruct((n_x * n_y, n_z, tall, width), bf16),
            jax.ShapeDtypeStruct((n_x * n_y, n_z, tall, width), f32),
        ],
        in_specs=[
            pl.BlockSpec(memory_space=pltpu.SMEM),
            by_row,
            by_row,
            by_row,
            pl.BlockSpec((block, 1), lambda i: (i, 0)),
            pl.BlockSpec((depth, block), lambda i: (0, i)),
        ],
        out_specs=[by_row, whole, whole],
        scratch_shapes=[pltpu.VMEM((depth, width), f32)],
        compiler_params=pltpu.CompilerParams(vmem_limit_bytes=40 << 20),
        cost_estimate=pl.CostEstimate(
            flops=2 * rows * depth * width, bytes_accessed=16 * rows * width + 6 * depth * width, transcendentals=rows
        ),
        name="finish",
    )(c.reshape(1), base, from_high, unit_rows, radius, text_t)


def slots_of(named, values, capacity):
    visits = named.shape[-1]
    order = jnp.arange(visits, dtype=jnp.int32)
    before = (order[:, None] < order[None, :]).astype(bf16)
    rank = jnp.dot(named.astype(bf16), before, preferred_element_type=f32)
    hit = named[..., None, :] & (rank[..., None, :] == jnp.arange(capacity, dtype=f32)[:, None])
    return jnp.sum(jnp.where(hit, values[..., None, :] + 1, 0), axis=-1) - 1


def route(owners, blocks, capacity):
    n_blocks, hard = owners.shape
    visits = n_blocks * hard
    n_x, n_c, n_h, n_l, n_y = (lax.axis_size(a) for a in ALL)
    x, c, zh, zl, y = (lax.axis_index(a) for a in ALL)
    n_z, devices = n_h * n_l, n_x * n_c * n_h * n_l * n_y
    xs, cs, ys = jnp.arange(n_x), jnp.arange(n_c), jnp.arange(n_y)
    z_at = zh * n_l + zl
    dest = (((xs[:, None, None] * n_c + cs[None, :, None]) * n_z) + z_at) * n_y + ys[None, None, :]
    dest = dest.reshape(-1, 1)
    me = ((x * n_c + c) * n_z + z_at) * n_y + y
    text_block = jnp.arange(visits, dtype=jnp.int32) // hard
    mine = owners.reshape(1, visits)
    first = slots_of(mine == dest, text_block[None], capacity).reshape(-1)

    pad = -(2 * visits) % 1024
    own = jnp.concatenate([owners.reshape(-1), blocks.reshape(-1), jnp.zeros((pad,), jnp.int32)])
    table = jnp.broadcast_to(own.reshape(1, -1, 128), (devices, own.shape[0] // 128, 128))
    table = lax.all_to_all(table, ALL, split_axis=0, concat_axis=0, tiled=True)
    table = table.reshape(n_x, n_c, n_h, n_l, n_y, -1)
    table = jnp.where(zh == 0, table, jnp.flip(table, 2))
    table = jnp.where(zl == 0, table, jnp.flip(table, 3))
    table = table.transpose(2, 3, 0, 1, 4, 5).reshape(n_z, n_x * n_c * n_y, -1)
    plane_at = (x * n_c + c) * n_y + y
    column = lax.dynamic_index_in_dim(table, plane_at, 1, keepdims=False)[1:, None, :visits]
    others = slots_of(column == dest, text_block, capacity).reshape(n_z - 1, -1)
    tags = slots_of(table[:, :, :visits] == me, table[:, :, visits : 2 * visits], capacity).reshape(n_z, -1)
    return [first] + [others[k] for k in range(n_z - 1)], jnp.maximum(tags, 0)


def gather_weight(proj):
    n_x, n_c, n_h, n_l, n_y = (lax.axis_size(a) for a in ALL)
    x, c, zh, zl, y = (lax.axis_index(a) for a in ALL)
    rows, width = proj.shape
    n_z, n_xy = n_h * n_l, n_x * n_y
    piece = jnp.pad(proj.astype(bf16), ((0, -rows % 8), (0, 0)))[None]
    column = [piece]
    for k in range(1, n_z):
        column.append(lax.ppermute(piece, COLUMN, [(i, i ^ k) for i in range(n_z)]))
    piece = jnp.concatenate(column)
    flat = [piece]
    for k in range(1, n_xy):
        flat.append(lax.ppermute(piece, ("x", "y"), [(i, i ^ k) for i in range(n_xy)]))
    piece = jnp.concatenate(flat)
    other = lax.ppermute(piece, "c", SWAP)
    piece = jnp.concatenate([piece, other])
    xs, cs, zs, ys = jnp.arange(n_x), jnp.arange(n_c), jnp.arange(n_z), jnp.arange(n_y)
    far_c = (cs ^ c)[None, :, None, None]
    far_xy = ((xs[:, None] * n_y + ys[None, :]) ^ (x * n_y + y))[:, None, None, :]
    far_z = (zs ^ (zh * n_l + zl))[None, None, :, None]
    at = ((far_c * n_xy + far_xy) * n_z + far_z).reshape(-1)
    return jnp.take(piece, at, axis=0)[:, :rows].reshape(-1, width)


def reduce_weight(send, keep, rows):
    n_xy, n_z, tall, width = send.shape
    other = lax.ppermute(send, "c", SWAP)
    total = (keep + other.astype(f32)).astype(bf16).reshape(n_xy, n_z * tall, width)
    total = lax.all_to_all(total, ("x", "y"), split_axis=0, concat_axis=0, tiled=True)
    total = jnp.sum(total.astype(f32), axis=0).reshape(n_z, tall, width).astype(bf16)
    total = lax.all_to_all(total, COLUMN, split_axis=0, concat_axis=0, tiled=True)
    return jnp.sum(total.astype(f32), axis=0)[:rows]


def step(text_feats, proj, first_moment, second_moment, owners, blocks, positives, bank):
    devices = lax.axis_size(ALL)
    plane = lax.axis_size(PLANE)
    rows_dev, _ = text_feats.shape
    text_blocks, hard = owners.shape
    tb = rows_dev // text_blocks
    visits = text_blocks * hard
    capacity = max(2, visits // devices + 1)

    text_high = lax.ppermute(text_feats, "zh", SWAP)
    text_low = lax.ppermute(text_feats, "zl", SWAP)
    text_far = lax.ppermute(text_high, "zl", SWAP)
    sources, tags = route(owners, blocks, capacity)
    text_far, weight_half, tags = lax.optimization_barrier((text_far, gather_weight(proj), tags))
    texts = (text_feats, text_low, text_high, text_far)

    def exchange(rows):
        rows = rows.reshape(plane, capacity * tb, -1)
        rows = lax.all_to_all(rows, PLANE, split_axis=0, concat_axis=0, tiled=True)
        return rows.reshape(plane * capacity * tb, -1)

    picks, got, replies, partial = [], [], [], []
    for k in range(4):
        row_of = sources[k][:, None] * tb + jnp.arange(tb, dtype=jnp.int32)[None, :]
        row_of = jnp.where(sources[k][:, None] >= 0, row_of, -1).reshape(-1)
        pick = (row_of[:, None] == jnp.arange(rows_dev, dtype=jnp.int32)[None, :]).astype(bf16)
        sent = jnp.dot(pick, texts[k], preferred_element_type=f32).astype(bf16)
        picks.append(pick)
        got.append(exchange(sent))
    replies += answer(got[:3], tags[:3].reshape(-1), weight_half, bank, tb)
    replies += answer(got[3:], tags[3], weight_half, bank, tb)
    for k in range(4):
        reply = exchange(replies[k])
        partial.append(
            lax.dot_general(picks[k], reply, (((0,), (0,)), ((), ())), preferred_element_type=f32)
        )
    from_far = lax.ppermute(partial[3].astype(bf16), "zl", SWAP)
    from_high = lax.ppermute((partial[2] + from_far.astype(f32)).astype(bf16), "zh", SWAP)
    from_low = lax.ppermute(partial[1].astype(bf16), "zl", SWAP)
    projected = jnp.dot(text_feats, weight_half, preferred_element_type=f32)
    radius = jnp.sqrt(jnp.sum(projected * projected, axis=-1, keepdims=True) + norm_eps)
    unit_rows = projected / radius
    unit_half = unit_rows.astype(bf16)
    scores = logit_scale * jnp.dot(unit_half, bank.T, preferred_element_type=f32) + logit_bias
    columns = jnp.arange(bank.shape[0], dtype=jnp.int32)
    labels = jnp.where(columns[None, :] == positives[:, None], 1.0, -1.0).astype(f32)
    local_coef = (-labels * jax.nn.sigmoid(-labels * scores)).astype(bf16)
    local_grad = logit_scale * jnp.dot(local_coef, bank, preferred_element_type=f32)
    local_grad, unit_rows, radius = lax.optimization_barrier((local_grad, unit_rows, radius))

    base = local_grad + partial[0] + from_low.astype(f32)
    n_x, n_z, n_y = lax.axis_size("x"), lax.axis_size(COLUMN), lax.axis_size("y")
    proj_grad_rows, send, keep = finish(
        lax.axis_index("c").astype(jnp.int32), base, from_high, unit_rows, radius, text_feats.T, n_x, n_z, n_y
    )
    weight_grad = reduce_weight(send, keep, proj.shape[0])
    text_grad = lax.dot_general(
        proj_grad_rows, weight_half, (((1,), (1,)), ((), ())), preferred_element_type=f32
    ).astype(bf16)
    new_first = beta_one * first_moment + (1.0 - beta_one) * weight_grad
    new_second = beta_two * second_moment + (1.0 - beta_two) * weight_grad * weight_grad
    first_hat = new_first / (1.0 - beta_one**adam_step)
    second_hat = new_second / (1.0 - beta_two**adam_step)
    new_proj = proj - learn_rate * (first_hat / (jnp.sqrt(second_hat) + adam_eps) + decay_rate * proj)
    return (text_grad, new_proj, new_first, new_second)


def solution(mesh):
    n_gx, n_gy = mesh.shape["gx"], mesh.shape["gy"]
    fine = Mesh(mesh.devices.reshape(n_gx // 2, 2, 2, 2, n_gy // 4), ALL)
    rows = P(ALL, None)
    return jax.shard_map(
        step,
        mesh=fine,
        in_specs=(rows, rows, rows, rows, rows, rows, P(ALL), rows),
        out_specs=(rows, rows, rows, rows),
        check_vma=False,
    )
```

profile of v0, /device:TPU:0, one launch (start us, length us, event | category | flops | bytes accessed | tf_op | source)
XLA Modules:
  0.0 405.1 jit_solution(6216333084682066105)
XLA Ops:
  0.6 0.9 convert_element_type.65
  1.6 3.1 collective-permute-start.2
  4.7 2.6 collective-permute-start.3
  7.3 1.9 collective-permute-start
  9.2 2.5 collective-permute-start.9
  14.2 2.8 all-to-all-start
  19.8 3.8 convolution_convert_fusion.3
  23.6 16.4 %collective-permute-done.3 = bf16[1,40,1152]{2,1,0:T(8,128)(2,1)S(1)} collective-permute-done((bf16[1,40,1152]{2,1,0:T(8,128)(2,1)S(1)}, bf16[1,40,1152]{2,1,0:T(8,128)(2,1)S(1)}, u32[]{:S(2)}, u32[]{:S(2)}) %collective-permute-start.3) | collective-permute-done | bytes 92192 | tf_op jit(solution)/shard_map/ppermute | solution.py:274
  40.8 1.5 collective-permute-start.5
  42.3 1.5 collective-permute-start.6
  46.4 23.9 %all-to-all-done = s32[32,8,128]{2,1,0:T(8,128)S(1)} async-done(((s32[32,8,128]{2,1,0:T(8,128)}), s32[32,8,128]{2,1,0:T(8,128)S(1)}, u32[]{:S(2)}, u32[]{:S(2)}) %all-to-all-start) | async-done | bytes 131104 | tf_op jit(solution)/shard_map/all_to_all | solution.py:254
  70.3 3.6 all-to-all-start.1
  76.6 0.9 constant_dynamic-update-slice_fusion.2
  77.5 3.8 convolution_convert_fusion.2
  81.3 14.8 %all-to-all-done.1 = bf16[8,96,1152]{2,1,0:T(8,128)(2,1)S(1)} async-done(((bf16[8,96,1152]{2,1,0:T(8,128)(2,1)}), bf16[8,96,1152]{2,1,0:T(8,128)(2,1)S(1)}, u32[]{:S(2)}, u32[]{:S(2)}) %all-to-all-start.1) | async-done | bytes 1769504 | tf_op jit(solution)/shard_map/all_to_all | solution.py:318
  96.1 1.2 copy-done.4
  97.3 3.6 all-to-all-start.2
  100.9 2.0 constant_dynamic-update-slice_fusion.1
  102.9 1.9 constant_dynamic-update-slice_fusion
  106.0 3.9 convolution_convert_fusion.1
  109.8 13.2 %all-to-all-done.2 = bf16[8,96,1152]{2,1,0:T(8,128)(2,1)S(1)} async-done(((bf16[8,96,1152]{2,1,0:T(8,128)(2,1)}), bf16[8,96,1152]{2,1,0:T(8,128)(2,1)S(1)}, u32[]{:S(2)}, u32[]{:S(2)}) %all-to-all-start.2) | async-done | bytes 1769504 | tf_op jit(solution)/shard_map/all_to_all | solution.py:318
  123.1 1.2 copy-done.5
  124.3 4.3 %all-to-all-start.3 = ((bf16[8,96,1152]{2,1,0:T(8,128)(2,1)}), bf16[8,96,1152]{2,1,0:T(8,128)(2,1)}, u32[]{:S(2)}, u32[]{:S(2)}) async-start(bf16[8,96,1152]{2,1,0:T(8,128)(2,1)} %bitcast.12), calls=%async_computation.3 | async-start | bytes 3538944 | tf_op jit(solution)/shard_map/all_to_all | solution.py:318
  129.1 1.1 collective-permute-start.1
  130.4 1.2 constant_dynamic-update-slice_fusion.7
  131.7 2.9 gather_fusion
  134.5 1.9 slice_select_fusion
  136.5 5.2 %reshape.478.refs_3_.refs_1_ = bf16[1152,1152]{1,0:T(8,128)(2,1)} reshape(bf16[32,36,1152]{2,1,0:T(8,128)(2,1)} %slice_select_fusion) | data formatting | bytes 5308416 | tf_op jit(solution)/shard_map/reshape | solution.py:287
  141.7 16.1 %collective-permute-done.1 = bf16[512,1152]{1,0:T(8,128)(2,1)} collective-permute-done((bf16[512,1152]{1,0:T(8,128)(2,1)}, bf16[512,1152]{1,0:T(8,128)(2,1)}, u32[]{:S(2)}, u32[]{:S(2)}) %collective-permute-start.1) | collective-permute-done | bytes 1179680 | tf_op jit(solution)/shard_map/ppermute | solution.py:311
  157.7 3.7 convolution_convert_fusion
  161.5 3.8 all-to-all-start.7
  165.9 35.1 %answer.2 = (bf16[768,1152]{1,0:T(8,128)(2,1)}, bf16[768,1152]{1,0:T(8,128)(2,1)}, bf16[768,1152]{1,0:T(8,128)(2,1)}) custom-call(s32[144]{0:T(256)} %reshape.483.tags_ref, bf16[768,1152]{1,0:T(8,128)(2,1)} %bitcast.62, bf16[768,1152]{1,0:T(8,128)(2,1)} %bitcast.63, bf16[768,1152]{1,0:T(8,128)(2,1)} %bitcast.13.refs_2_, ...), custom_call_target="tpu_custom_call" | custom-call | flops 11551113216 | bytes 20348928 | tf_op jit(solution)/shard_map/answer/pallas_call | solution.py:132
  201.0 1.3 copy-done.8
  202.3 3.8 all-to-all-start.5
  206.6 17.4 %answer.3 = bf16[768,1152]{1,0:T(8,128)(2,1)} custom-call(s32[48]{0:T(128)} %slice_bitcast_fusion.tags_ref, bf16[768,1152]{1,0:T(8,128)(2,1)} %bitcast.67, bf16[1152,1152]{1,0:T(8,128)(2,1)} %reshape.478.refs_3_.refs_1_, bf16[3072,1152]{1,0:T(8,128)(2,1)} %refs_2_.1), custom_call_target="tpu_custom_call" | custom-call | flops 3850371072 | bytes 13271040 | tf_op jit(solution)/shard_map/answer/pallas_call | solution.py:132
  224.0 4.2 %all-to-all-done.5 = bf16[8,96,1152]{2,1,0:T(8,128)(2,1)S(1)} async-done(((bf16[8,96,1152]{2,1,0:T(8,128)(2,1)}), bf16[8,96,1152]{2,1,0:T(8,128)(2,1)S(1)}, u32[]{:S(2)}, u32[]{:S(2)}) %all-to-all-start.5) | async-done | bytes 1769504 | tf_op jit(solution)/shard_map/all_to_all | solution.py:318
  228.2 1.3 copy-done.6
  229.5 3.6 all-to-all-start.8
  233.1 1.6 copy.33
  234.7 20.6 %all-to-all-done.8 = bf16[8,96,1152]{2,1,0:T(8,128)(2,1)S(1)} async-done(((bf16[8,96,1152]{2,1,0:T(8,128)(2,1)}), bf16[8,96,1152]{2,1,0:T(8,128)(2,1)S(1)}, u32[]{:S(2)}, u32[]{:S(2)}) %all-to-all-start.8) | async-done | bytes 1769504 | tf_op jit(solution)/shard_map/all_to_all | solution.py:318
  255.3 1.2 copy-done.9
  256.5 4.3 %all-to-all-start.6 = ((bf16[8,96,1152]{2,1,0:T(8,128)(2,1)}), bf16[8,96,1152]{2,1,0:T(8,128)(2,1)}, u32[]{:S(2)}, u32[]{:S(2)}) async-start(bf16[8,96,1152]{2,1,0:T(8,128)(2,1)} %bitcast.18), calls=%async_computation.6 | async-start | bytes 3538944 | tf_op jit(solution)/shard_map/all_to_all | solution.py:318
  260.8 3.8 multiply_reduce_fusion
  264.7 2.0 copy.24
  266.6 4.0 convolution_convert_fusion.4
  270.6 2.3 collective-permute-start.11
  273.2 1.2 copy-done.7
  274.4 2.4 convolution_convert_fusion.5
  276.8 6.3 %all-to-all-done.6 = bf16[8,96,1152]{2,1,0:T(8,128)(2,1)} async-done(((bf16[8,96,1152]{2,1,0:T(8,128)(2,1)}), bf16[8,96,1152]{2,1,0:T(8,128)(2,1)}, u32[]{:S(2)}, u32[]{:S(2)}) %all-to-all-start.6) | async-done | bytes 1769504 | tf_op jit(solution)/shard_map/all_to_all | solution.py:318
  283.1 4.7 %all-to-all-start.4 = ((bf16[8,96,1152]{2,1,0:T(8,128)(2,1)}), bf16[8,96,1152]{2,1,0:T(8,128)(2,1)}, u32[]{:S(2)}, u32[]{:S(2)}) async-start(bf16[8,96,1152]{2,1,0:T(8,128)(2,1)} %bitcast.64), calls=%async_computation.4 | async-start | bytes 3538944 | tf_op jit(solution)/shard_map/all_to_all | solution.py:318
  287.8 12.3 %collective-permute-done.11 = bf16[512,1152]{1,0:T(8,128)(2,1)} collective-permute-done((bf16[512,1152]{1,0:T(8,128)(2,1)}, bf16[512,1152]{1,0:T(8,128)(2,1)}, u32[]{:S(2)}, u32[]{:S(2)}) %collective-permute-start.11) | collective-permute-done | bytes 1179680 | tf_op jit(solution)/shard_map/ppermute | solution.py:336
  300.1 4.2 %add_convert_fusion.1 = bf16[512,1152]{1,0:T(8,128)(2,1)} fusion(bf16[512,1152]{1,0:T(8,128)(2,1)} %collective-permute-done.11, bf16[768,1152]{1,0:T(8,128)(2,1)} %bitcast.19, s32[768]{0:T(1024)S(1)} %copy-done.16), kind=kOutput, calls=%fused_computation.14 | convolution fusion | flops 908132352 | bytes 4131840 | tf_op jit(solution)/shard_map/dot_general | solution.py:334
  304.3 2.7 collective-permute-start.12
  307.0 15.6 %convolution_multiply_fusion = f32[512,1152]{1,0:T(8,128)} fusion(bf16[3072,1152]{1,0:T(8,128)(2,1)} %refs_2_.1, s32[512]{0:T(512)S(1)} %copy-done.21, f32[512,1152]{1,0:T(8,128)S(1)} %divide_bitcast_fusion.unit_ref), kind=kOutput, calls=%fused_computation.3 | convolution fusion | flops 7266238464 | bytes 11798528 | tf_op jit(solution)/shard_map/dot_general | solution.py:347
  323.4 21.0 %collective-permute-done.10 = bf16[512,1152]{1,0:T(8,128)(2,1)} collective-permute-done((bf16[512,1152]{1,0:T(8,128)(2,1)}, bf16[512,1152]{1,0:T(8,128)(2,1)}, u32[]{:S(2)}, u32[]{:S(2)}) %collective-permute-start.10) | collective-permute-done | bytes 1179680 | tf_op jit(solution)/shard_map/ppermute | solution.py:338
  344.5 3.9 convert_add_fusion.base_ref
  348.4 9.8 %collective-permute-done.12.high_ref = bf16[512,1152]{1,0:T(8,128)(2,1)} collective-permute-done((bf16[512,1152]{1,0:T(8,128)(2,1)}, bf16[512,1152]{1,0:T(8,128)(2,1)}, u32[]{:S(2)}, u32[]{:S(2)}) %collective-permute-start.12) | collective-permute-done | bytes 1179680 | tf_op jit(solution)/shard_map/ppermute | solution.py:337
  358.2 4.7 %finish.1 = (bf16[512,1152]{1,0:T(8,128)(2,1)S(1)}, bf16[4,4,40,1152]{3,2,1,0:T(8,128)(2,1)S(1)}, f32[4,4,40,1152]{3,2,1,0:T(8,128)S(1)}) custom-call(s32[1]{0:T(128)} %bitcast.c_ref, f32[512,1152]{1,0:T(8,128)S(1)} %convert_add_fusion.base_ref, bf16[512,1152]{1,0:T(8,128)(2,1)} %collective-permute-done.12.high_ref, ...), custom_call_target="tpu_custom_call" | custom-call | flops 1358954496 | bytes 17399808 | tf_op jit(solution)/shard_map/finish/pallas_call | solution.py:201
  363.0 3.3 collective-permute-done.13
  366.6 22.6 %all_to_all.55 = bf16[4,160,1152]{2,1,0:T(8,128)(2,1)S(1)} all-to-all(bf16[4,160,1152]{2,1,0:T(8,128)(2,1)S(1)} %bitcast.61), channel_id=1, replica_groups=mesh['x'=2,'c'=2,'zh'=2,'zl'=2,'y'=2] {'x','y'}, dimensions={0} | all-to-all | bytes 2949120 | tf_op jit(solution)/shard_map/all_to_all | solution.py:294
  389.2 1.1 reduce_sum.61
  390.3 3.5 all-to-all-start.10
  393.8 4.7 %convolution_convert_fusion.6 = bf16[512,1152]{1,0:T(8,128)(2,1)} fusion(bf16[512,1152]{1,0:T(8,128)(2,1)S(1)} %copy-done.2, bf16[1152,1152]{1,0:T(8,128)(2,1)} %reshape.478.refs_3_.refs_1_), kind=kOutput, calls=%fused_computation.11 | convolution fusion | flops 1359544320 | bytes 5013504 | tf_op jit(solution)/shard_map/dot_general | solution.py:356
  398.5 5.7 %all-to-all-done.10 = bf16[4,40,1152]{2,1,0:T(8,128)(2,1)S(1)} async-done(((bf16[4,40,1152]{2,1,0:T(8,128)(2,1)}), bf16[4,40,1152]{2,1,0:T(8,128)(2,1)S(1)}, u32[]{:S(2)}, u32[]{:S(2)}) %all-to-all-start.10) | async-done | bytes 368672 | tf_op jit(solution)/shard_map/all_to_all | solution.py:296
  (138 shorter events, 16.6 us)
Async XLA Ops:
  1.6 22.0 %collective-permute-start.2 = (bf16[1,40,1152]{2,1,0:T(8,128)(2,1)S(1)}, bf16[1,40,1152]{2,1,0:T(8,128)(2,1)S(1)}, u32[]{:S(2)}, u32[]{:S(2)}) collective-permute-start(bf16[1,40,1152]{2,1,0:T(8,128)(2,1)S(1)} %pad_bitcast_fusion), channel_id=1, source_target_pairs={{0,2},{2,0},{4,6},{6,4},{1,3},{3,1},{5,7},{7,5},{8,10},{10,8},{12,... | collective-permute-start | bytes 276488 | tf_op jit(solution)/shard_map/ppermute | solution.py:274
  4.7 35.3 %collective-permute-start.3 = (bf16[1,40,1152]{2,1,0:T(8,128)(2,1)S(1)}, bf16[1,40,1152]{2,1,0:T(8,128)(2,1)S(1)}, u32[]{:S(2)}, u32[]{:S(2)}) collective-permute-start(bf16[1,40,1152]{2,1,0:T(8,128)(2,1)S(1)} %pad_bitcast_fusion), channel_id=1, source_target_pairs={{0,4},{2,6},{4,0},{6,2},{1,5},{3,7},{5,1},{7,3},{8,12},{10,14},{12... | collective-permute-start | bytes 276488 | tf_op jit(solution)/shard_map/ppermute | solution.py:274
  7.3 32.7 %collective-permute-start.4 = (bf16[1,40,1152]{2,1,0:T(8,128)(2,1)S(1)}, bf16[1,40,1152]{2,1,0:T(8,128)(2,1)S(1)}, u32[]{:S(2)}, u32[]{:S(2)}) collective-permute-start(bf16[1,40,1152]{2,1,0:T(8,128)(2,1)S(1)} %pad_bitcast_fusion), channel_id=1, source_target_pairs={{0,6},{2,4},{4,2},{6,0},{1,7},{3,5},{5,3},{7,1},{8,14},{10,12},{12... | collective-permute-start | bytes 276488 | tf_op jit(solution)/shard_map/ppermute | solution.py:274
  7.3 98.7 %collective-permute-start = (bf16[512,1152]{1,0:T(8,128)(2,1)}, bf16[512,1152]{1,0:T(8,128)(2,1)}, u32[]{:S(2)}, u32[]{:S(2)}) collective-permute-start(bf16[512,1152]{1,0:T(8,128)(2,1)} %param.8), channel_id=1, source_target_pairs={{0,4},{4,0},{1,5},{5,1},{2,6},{6,2},{3,7},{7,3},{8,12},{12,8},{9,1... | collective-permute-start | bytes 3538952 | tf_op jit(solution)/shard_map/ppermute | solution.py:309
  9.2 68.3 %collective-permute-start.9 = (bf16[512,1152]{1,0:T(8,128)(2,1)}, bf16[512,1152]{1,0:T(8,128)(2,1)}, u32[]{:S(2)}, u32[]{:S(2)}) collective-permute-start(bf16[512,1152]{1,0:T(8,128)(2,1)} %param.8), channel_id=1, source_target_pairs={{0,2},{2,0},{1,3},{3,1},{4,6},{6,4},{5,7},{7,5},{8,10},{10,8},{9,1... | collective-permute-start | bytes 3538952 | tf_op jit(solution)/shard_map/ppermute | solution.py:310
  14.2 56.1 %all-to-all-start = ((s32[32,8,128]{2,1,0:T(8,128)}), s32[32,8,128]{2,1,0:T(8,128)S(1)}, u32[]{:S(2)}, u32[]{:S(2)}) async-start(s32[32,8,128]{2,1,0:T(8,128)} %broadcast_in_dim.138), calls=%async_computation | async-start | bytes 262144 | tf_op jit(solution)/shard_map/all_to_all | solution.py:254
  40.8 35.8 %collective-permute-start.5 = (bf16[4,40,1152]{2,1,0:T(8,128)(2,1)}, bf16[4,40,1152]{2,1,0:T(8,128)(2,1)S(1)}, u32[]{:S(2)}, u32[]{:S(2)}) collective-permute-start(bf16[4,40,1152]{2,1,0:T(8,128)(2,1)} %pad_maximum_fusion), channel_id=1, source_target_pairs={{0,1},{1,0},{16,17},{17,16},{2,3},{3,2},{18,19},{19,18},{4,5},{5,4... | collective-permute-start | bytes 1105928 | tf_op jit(solution)/shard_map/ppermute | solution.py:278
  42.3 58.6 %collective-permute-start.6 = (bf16[4,40,1152]{2,1,0:T(8,128)(2,1)}, bf16[4,40,1152]{2,1,0:T(8,128)(2,1)}, u32[]{:S(2)}, u32[]{:S(2)}) collective-permute-start(bf16[4,40,1152]{2,1,0:T(8,128)(2,1)} %pad_maximum_fusion), channel_id=1, source_target_pairs={{0,16},{1,17},{16,0},{17,1},{2,18},{3,19},{18,2},{19,3},{4,20},{5,... | collective-permute-start | bytes 1105928 | tf_op jit(solution)/shard_map/ppermute | solution.py:278
  43.8 59.1 %collective-permute-start.7 = (bf16[4,40,1152]{2,1,0:T(8,128)(2,1)}, bf16[4,40,1152]{2,1,0:T(8,128)(2,1)}, u32[]{:S(2)}, u32[]{:S(2)}) collective-permute-start(bf16[4,40,1152]{2,1,0:T(8,128)(2,1)} %pad_maximum_fusion), channel_id=1, source_target_pairs={{0,17},{1,16},{16,1},{17,0},{2,19},{3,18},{18,3},{19,2},{4,21},{5,... | collective-permute-start | bytes 1105928 | tf_op jit(solution)/shard_map/ppermute | solution.py:278
  70.3 25.8 %all-to-all-start.1 = ((bf16[8,96,1152]{2,1,0:T(8,128)(2,1)}), bf16[8,96,1152]{2,1,0:T(8,128)(2,1)S(1)}, u32[]{:S(2)}, u32[]{:S(2)}) async-start(bf16[8,96,1152]{2,1,0:T(8,128)(2,1)} %bitcast.8), calls=%async_computation.1 | async-start | bytes 3538944 | tf_op jit(solution)/shard_map/all_to_all | solution.py:318
  74.2 7.1 %copy-start.11 = (s32[4,8,1024]{2,1,0:T(8,128)}, s32[4,8,1024]{2,1,0:T(8,128)S(1)}, u32[]{:S(2)}) copy-start(s32[4,8,1024]{2,1,0:T(8,128)S(1)} %reshape.482) | copy-start | bytes 393220
  76.0 5.2 %copy-start.17 = (s32[768]{0:T(1024)}, s32[768]{0:T(1024)S(1)}, u32[]{:S(2)}) copy-start(s32[768]{0:T(1024)S(1)} %select_n.124) | copy-start | bytes 9220
  76.6 29.4 %copy-start.15 = (s32[768]{0:T(1024)}, s32[768]{0:T(1024)S(1)}, u32[]{:S(2)}) copy-start(s32[768]{0:T(1024)S(1)} %select_n.126) | copy-start | bytes 9220
  96.1 1.2 copy-start.4
  97.3 25.8 %all-to-all-start.2 = ((bf16[8,96,1152]{2,1,0:T(8,128)(2,1)}), bf16[8,96,1152]{2,1,0:T(8,128)(2,1)S(1)}, u32[]{:S(2)}, u32[]{:S(2)}) async-start(bf16[8,96,1152]{2,1,0:T(8,128)(2,1)} %bitcast.65), calls=%async_computation.2 | async-start | bytes 3538944 | tf_op jit(solution)/shard_map/all_to_all | solution.py:318
  100.9 4.3 %copy-start.12 = (s32[4,8,1024]{2,1,0:T(8,128)S(1)}, s32[4,8,1024]{2,1,0:T(8,128)}, u32[]{:S(2)}) copy-start(s32[4,8,1024]{2,1,0:T(8,128)} %copy-done.11) | copy-start | bytes 393220
  104.8 25.6 %collective-permute-start.8 = (bf16[16,40,1152]{2,1,0:T(8,128)(2,1)}, bf16[16,40,1152]{2,1,0:T(8,128)(2,1)S(1)}, u32[]{:S(2)}, u32[]{:S(2)}) collective-permute-start(bf16[16,40,1152]{2,1,0:T(8,128)(2,1)} %get-tuple-element.31), channel_id=1, source_target_pairs={{0,8},{8,0},{1,9},{9,1},{2,10},{10,2},{3,11},{11,3},{4,12},{12,4},... | collective-permute-start | bytes 4423688 | tf_op jit(solution)/shard_map/ppermute | solution.py:280
  123.1 1.2 copy-start.5
  123.1 5.9 %copy-start.19 = (pred[1,8,6]{1,2,0:T(8,128)(4,1)S(1)}, pred[1,8,6]{1,2,0:T(8,128)(4,1)}, u32[]{:S(2)}) copy-start(pred[1,8,6]{1,2,0:T(8,128)(4,1)} %get-tuple-element.45) | copy-start | bytes 148
  124.3 37.2 %all-to-all-start.3 = ((bf16[8,96,1152]{2,1,0:T(8,128)(2,1)}), bf16[8,96,1152]{2,1,0:T(8,128)(2,1)}, u32[]{:S(2)}, u32[]{:S(2)}) async-start(bf16[8,96,1152]{2,1,0:T(8,128)(2,1)} %bitcast.12), calls=%async_computation.3 | async-start | bytes 3538944 | tf_op jit(solution)/shard_map/all_to_all | solution.py:318
  129.1 28.6 %collective-permute-start.1 = (bf16[512,1152]{1,0:T(8,128)(2,1)}, bf16[512,1152]{1,0:T(8,128)(2,1)}, u32[]{:S(2)}, u32[]{:S(2)}) collective-permute-start(bf16[512,1152]{1,0:T(8,128)(2,1)} %collective-permute-done), channel_id=1, source_target_pairs={{0,2},{2,0},{1,3},{3,1},{4,6},{6,4},{5,7},{7,5},{8,10},{10,8},{9,1... | collective-permute-start | bytes 3538952 | tf_op jit(solution)/shard_map/ppermute | solution.py:311
  131.7 2.9 copy-start.20
  161.5 39.6 %all-to-all-start.7 = ((bf16[8,96,1152]{2,1,0:T(8,128)(2,1)}), bf16[8,96,1152]{2,1,0:T(8,128)(2,1)S(1)}, u32[]{:S(2)}, u32[]{:S(2)}) async-start(bf16[8,96,1152]{2,1,0:T(8,128)(2,1)} %bitcast.21), calls=%async_computation.7 | async-start | bytes 3538944 | tf_op jit(solution)/shard_map/all_to_all | solution.py:318
  201.0 1.3 copy-start.8
  202.3 25.9 %all-to-all-start.5 = ((bf16[8,96,1152]{2,1,0:T(8,128)(2,1)}), bf16[8,96,1152]{2,1,0:T(8,128)(2,1)S(1)}, u32[]{:S(2)}, u32[]{:S(2)}) async-start(bf16[8,96,1152]{2,1,0:T(8,128)(2,1)} %bitcast.68), calls=%async_computation.5 | async-start | bytes 3538944 | tf_op jit(solution)/shard_map/all_to_all | solution.py:318
  228.2 1.3 copy-start.6
  229.5 25.8 %all-to-all-start.8 = ((bf16[8,96,1152]{2,1,0:T(8,128)(2,1)}), bf16[8,96,1152]{2,1,0:T(8,128)(2,1)S(1)}, u32[]{:S(2)}, u32[]{:S(2)}) async-start(bf16[8,96,1152]{2,1,0:T(8,128)(2,1)} %bitcast.70), calls=%async_computation.8 | async-start | bytes 3538944 | tf_op jit(solution)/shard_map/all_to_all | solution.py:318
  255.3 1.2 copy-start.9
  256.5 26.6 %all-to-all-start.6 = ((bf16[8,96,1152]{2,1,0:T(8,128)(2,1)}), bf16[8,96,1152]{2,1,0:T(8,128)(2,1)}, u32[]{:S(2)}, u32[]{:S(2)}) async-start(bf16[8,96,1152]{2,1,0:T(8,128)(2,1)} %bitcast.18), calls=%async_computation.6 | async-start | bytes 3538944 | tf_op jit(solution)/shard_map/all_to_all | solution.py:318
  266.6 6.3 %copy-start.3 = (f32[1152,512]{0,1:T(8,128)S(1)}, f32[1152,512]{0,1:T(8,128)}, u32[]{:S(2)}) copy-start(f32[1152,512]{0,1:T(8,128)} %copy.24) | copy-start | bytes 7077892
  270.6 29.4 %collective-permute-start.11 = (bf16[512,1152]{1,0:T(8,128)(2,1)}, bf16[512,1152]{1,0:T(8,128)(2,1)}, u32[]{:S(2)}, u32[]{:S(2)}) collective-permute-start(bf16[512,1152]{1,0:T(8,128)(2,1)} %convolution_convert_fusion.4), channel_id=1, source_target_pairs={{0,2},{2,0},{1,3},{3,1},{4,6},{6,4},{5,7},{7,5},{8,10},{10,8},{9,1... | collective-permute-start | bytes 3538952 | tf_op jit(solution)/shard_map/ppermute | solution.py:336
  273.0 1.5 copy-start.7
  273.0 1.5 copy-start.18
  276.8 67.7 %collective-permute-start.10 = (bf16[512,1152]{1,0:T(8,128)(2,1)}, bf16[512,1152]{1,0:T(8,128)(2,1)}, u32[]{:S(2)}, u32[]{:S(2)}) collective-permute-start(bf16[512,1152]{1,0:T(8,128)(2,1)} %convolution_convert_fusion.5), channel_id=1, source_target_pairs={{0,2},{2,0},{1,3},{3,1},{4,6},{6,4},{5,7},{7,5},{8,10},{10,8},{9,1... | collective-permute-start | bytes 3538952 | tf_op jit(solution)/shard_map/ppermute | solution.py:338
  283.1 17.0 %copy-start.16 = (s32[768]{0:T(1024)S(1)}, s32[768]{0:T(1024)}, u32[]{:S(2)}) copy-start(s32[768]{0:T(1024)} %copy-done.15) | copy-start | bytes 9220
  283.1 40.3 %all-to-all-start.4 = ((bf16[8,96,1152]{2,1,0:T(8,128)(2,1)}), bf16[8,96,1152]{2,1,0:T(8,128)(2,1)}, u32[]{:S(2)}, u32[]{:S(2)}) async-start(bf16[8,96,1152]{2,1,0:T(8,128)(2,1)} %bitcast.64), calls=%async_computation.4 | async-start | bytes 3538944 | tf_op jit(solution)/shard_map/all_to_all | solution.py:318
  300.1 6.9 %copy-start.21 = (s32[512]{0:T(512)S(1)}, s32[512]{0:T(512)}, u32[]{:S(2)}) copy-start(s32[512]{0:T(512)} %param.14) | copy-start | bytes 6148
  304.3 53.9 %collective-permute-start.12 = (bf16[512,1152]{1,0:T(8,128)(2,1)}, bf16[512,1152]{1,0:T(8,128)(2,1)}, u32[]{:S(2)}, u32[]{:S(2)}) collective-permute-start(bf16[512,1152]{1,0:T(8,128)(2,1)} %add_convert_fusion.1), channel_id=1, source_target_pairs={{0,4},{4,0},{1,5},{5,1},{2,6},{6,2},{3,7},{7,3},{8,12},{12,8},{9,1... | collective-permute-start | bytes 3538952 | tf_op jit(solution)/shard_map/ppermute | solution.py:337
  344.5 13.8 %copy-start = (f32[512,1]{1,0:T(8,128)S(1)}, f32[512,1]{1,0:T(8,128)}, u32[]{:S(2)}) copy-start(f32[512,1]{1,0:T(8,128)} %copy.34.radius_ref) | copy-start | bytes 6148
  362.9 3.6 copy-start.1
  363.0 3.3 collective-permute-start.13
  389.2 4.5 %copy-start.2 = (bf16[512,1152]{1,0:T(8,128)(2,1)S(1)}, bf16[512,1152]{1,0:T(8,128)(2,1)}, u32[]{:S(2)}) copy-start(bf16[512,1152]{1,0:T(8,128)(2,1)} %copy-done.1) | copy-start | bytes 3538948
  390.3 13.9 %all-to-all-start.10 = ((bf16[4,40,1152]{2,1,0:T(8,128)(2,1)}), bf16[4,40,1152]{2,1,0:T(8,128)(2,1)S(1)}, u32[]{:S(2)}, u32[]{:S(2)}) async-start(bf16[4,40,1152]{2,1,0:T(8,128)(2,1)} %bitcast.27), calls=%async_computation.10 | async-start | bytes 737280 | tf_op jit(solution)/shard_map/all_to_all | solution.py:296
  393.8 10.5 %copy-start.10 = (f32[36,1152]{1,0:T(8,128)S(1)}, f32[36,1152]{1,0:T(8,128)}, u32[]{:S(2)}) copy-start(f32[36,1152]{1,0:T(8,128)} %param.9) | copy-start | bytes 497668
  393.8 10.5 %copy-start.13 = (f32[36,1152]{1,0:T(8,128)S(1)}, f32[36,1152]{1,0:T(8,128)}, u32[]{:S(2)}) copy-start(f32[36,1152]{1,0:T(8,128)} %param.10) | copy-start | bytes 497668
  393.8 10.5 %copy-start.14 = (f32[36,1152]{1,0:T(8,128)S(1)}, f32[36,1152]{1,0:T(8,128)}, u32[]{:S(2)}) copy-start(f32[36,1152]{1,0:T(8,128)} %param.11) | copy-start | bytes 497668
where the time goes:
time: 407 us; the launch traced here: 405 us
  waiting for transfers between devices  168 us (41%)
  starting transfers between devices  58.1 us (14%)
  Pallas kernels  57.2 us (14%)
  matrix products  54.2 us (13%)
  local copies, waits for them, and re-layouts  34.8 us (9%)
  blocking collectives  22.6 us (6%)
  other arithmetic  9.43 us (2%)
    all_to_all x8, waiting for transfers between devices, exchange(): rows = lax.all_to_all(rows, PLANE, split_axis=0, concat_axis=0, tiled=True)  59.1 us
    pallas_call x2, Pallas kernels, answer(): pl.pallas_call(functools.partial(answer_kernel, groups, slots, tb, banks,...  52.4 us
    all_to_all x8, starting transfers between devices, exchange(): rows = lax.all_to_all(rows, PLANE, split_axis=0, concat_axis=0, tiled=True)  31.7 us
    all_to_all x1, waiting for transfers between devices, route(): table = lax.all_to_all(table, ALL, split_axis=0, concat_axis=0, tiled=True)  23.9 us
    all_to_all x1, blocking collectives, reduce_weight(): lax.all_to_all(total, ('x', 'y'), split_axis=0, concat_axis=0, tiled=True)  22.6 us
    ppermute x1, waiting for transfers between devices, step(): from_low = lax.ppermute(partial[1].astype(bf16), 'zl', SWAP)  21 us
    ppermute x3, waiting for transfers between devices, gather_weight(): column.append(lax.ppermute(piece, COLUMN, [(i, i ^ k) for i in range(n_z)]))  16.4 us
    unnamed x54, local copies, waits for them, and re-layouts  16.3 us
  transfers between devices with their start and end apart: 24, of which 13 were waited for; matrix products, arithmetic and copies ran while one was open for 22% of the time, Pallas kernels for 13%

commit v1 on v0

--- a/solution.py
+++ b/solution.py
@@ -233,46 +233,22 @@
     return jnp.sum(jnp.where(hit, values[..., None, :] + 1, 0), axis=-1) - 1
 
 
-def route(owners, blocks, capacity):
-    n_blocks, hard = owners.shape
-    visits = n_blocks * hard
-    n_x, n_c, n_h, n_l, n_y = (lax.axis_size(a) for a in ALL)
-    x, c, zh, zl, y = (lax.axis_index(a) for a in ALL)
-    n_z, devices = n_h * n_l, n_x * n_c * n_h * n_l * n_y
-    xs, cs, ys = jnp.arange(n_x), jnp.arange(n_c), jnp.arange(n_y)
-    z_at = zh * n_l + zl
-    dest = (((xs[:, None, None] * n_c + cs[None, :, None]) * n_z) + z_at) * n_y + ys[None, None, :]
-    dest = dest.reshape(-1, 1)
-    me = ((x * n_c + c) * n_z + z_at) * n_y + y
-    text_block = jnp.arange(visits, dtype=jnp.int32) // hard
-    mine = owners.reshape(1, visits)
-    first = slots_of(mine == dest, text_block[None], capacity).reshape(-1)
-
-    pad = -(2 * visits) % 1024
-    own = jnp.concatenate([owners.reshape(-1), blocks.reshape(-1), jnp.zeros((pad,), jnp.int32)])
-    table = jnp.broadcast_to(own.reshape(1, -1, 128), (devices, own.shape[0] // 128, 128))
-    table = lax.all_to_all(table, ALL, split_axis=0, concat_axis=0, tiled=True)
-    table = table.reshape(n_x, n_c, n_h, n_l, n_y, -1)
-    table = jnp.where(zh == 0, table, jnp.flip(table, 2))
-    table = jnp.where(zl == 0, table, jnp.flip(table, 3))
-    table = table.transpose(2, 3, 0, 1, 4, 5).reshape(n_z, n_x * n_c * n_y, -1)
-    plane_at = (x * n_c + c) * n_y + y
-    column = lax.dynamic_index_in_dim(table, plane_at, 1, keepdims=False)[1:, None, :visits]
-    others = slots_of(column == dest, text_block, capacity).reshape(n_z - 1, -1)
-    tags = slots_of(table[:, :, :visits] == me, table[:, :, visits : 2 * visits], capacity).reshape(n_z, -1)
-    return [first] + [others[k] for k in range(n_z - 1)], jnp.maximum(tags, 0)
-
-
-def gather_weight(proj):
+def gather_weight(proj, owners, blocks):
     n_x, n_c, n_h, n_l, n_y = (lax.axis_size(a) for a in ALL)
     x, c, zh, zl, y = (lax.axis_index(a) for a in ALL)
     rows, width = proj.shape
     n_z, n_xy = n_h * n_l, n_x * n_y
-    piece = jnp.pad(proj.astype(bf16), ((0, -rows % 8), (0, 0)))[None]
+    listed = jnp.concatenate([owners.reshape(-1), blocks.reshape(-1)]).astype(bf16)
+    entries = listed.shape[0]
+    list_rows = -(-entries // width)
+    listed = jnp.pad(listed, (0, list_rows * width - entries)).reshape(list_rows, width)
+    piece = jnp.concatenate([proj.astype(bf16), listed])
+    piece = jnp.pad(piece, ((0, -(rows + list_rows) % 8), (0, 0)))[None]
     column = [piece]
     for k in range(1, n_z):
         column.append(lax.ppermute(piece, COLUMN, [(i, i ^ k) for i in range(n_z)]))
     piece = jnp.concatenate(column)
+    column_lists = piece[:, rows : rows + list_rows].reshape(n_z, -1)[:, :entries].astype(jnp.int32)
     flat = [piece]
     for k in range(1, n_xy):
         flat.append(lax.ppermute(piece, ("x", "y"), [(i, i ^ k) for i in range(n_xy)]))
@@ -284,7 +260,31 @@
     far_xy = ((xs[:, None] * n_y + ys[None, :]) ^ (x * n_y + y))[:, None, None, :]
     far_z = (zs ^ (zh * n_l + zl))[None, None, :, None]
     at = ((far_c * n_xy + far_xy) * n_z + far_z).reshape(-1)
-    return jnp.take(piece, at, axis=0)[:, :rows].reshape(-1, width)
+    piece = jnp.take(piece, at, axis=0)
+    lists = piece[:, rows : rows + list_rows].reshape(piece.shape[0], -1)[:, :entries].astype(jnp.int32)
+    return piece[:, :rows].reshape(-1, width), column_lists, lists
+
+
+def route(owners, column_lists, lists, capacity):
+    n_blocks, hard = owners.shape
+    visits = n_blocks * hard
+    n_x, n_c, n_h, n_l, n_y = (lax.axis_size(a) for a in ALL)
+    x, c, zh, zl, y = (lax.axis_index(a) for a in ALL)
+    n_z = n_h * n_l
+    xs, cs, ys = jnp.arange(n_x), jnp.arange(n_c), jnp.arange(n_y)
+    z_at = zh * n_l + zl
+    dest = (((xs[:, None, None] * n_c + cs[None, :, None]) * n_z) + z_at) * n_y + ys[None, None, :]
+    dest = dest.reshape(-1, 1)
+    me = ((x * n_c + c) * n_z + z_at) * n_y + y
+    text_block = jnp.arange(visits, dtype=jnp.int32) // hard
+    first = slots_of(owners.reshape(1, visits) == dest, text_block[None], capacity).reshape(-1)
+    others = slots_of(column_lists[1:, None, :visits] == dest, text_block, capacity).reshape(n_z - 1, -1)
+    table = lists.reshape(n_x, n_c, n_h, n_l, n_y, -1)
+    table = jnp.where(zh == 0, table, jnp.flip(table, 2))
+    table = jnp.where(zl == 0, table, jnp.flip(table, 3))
+    table = table.transpose(2, 3, 0, 1, 4, 5).reshape(n_z, n_x * n_c * n_y, -1)
+    tags = slots_of(table[:, :, :visits] == me, table[:, :, visits:], capacity).reshape(n_z, -1)
+    return [first] + [others[k] for k in range(n_z - 1)], jnp.maximum(tags, 0)
 
 
 def reduce_weight(send, keep, rows):
@@ -306,11 +306,11 @@
     visits = text_blocks * hard
     capacity = max(2, visits // devices + 1)
 
+    text_low = lax.ppermute(text_feats, "zl", SWAP)
     text_high = lax.ppermute(text_feats, "zh", SWAP)
-    text_low = lax.ppermute(text_feats, "zl", SWAP)
     text_far = lax.ppermute(text_high, "zl", SWAP)
-    sources, tags = route(owners, blocks, capacity)
-    text_far, weight_half, tags = lax.optimization_barrier((text_far, gather_weight(proj), tags))
+    weight_half, column_lists, lists = gather_weight(proj, owners, blocks)
+    sources, tags = route(owners, column_lists, lists, capacity)
     texts = (text_feats, text_low, text_high, text_far)
 
     def exchange(rows):
@@ -326,7 +326,8 @@
         sent = jnp.dot(pick, texts[k], preferred_element_type=f32).astype(bf16)
         picks.append(pick)
         got.append(exchange(sent))
-    replies += answer(got[:3], tags[:3].reshape(-1), weight_half, bank, tb)
+    replies += answer(got[:2], tags[:2].reshape(-1), weight_half, bank, tb)
+    replies += answer(got[2:3], tags[2], weight_half, bank, tb)
     replies += answer(got[3:], tags[3], weight_half, bank, tb)
     for k in range(4):
         reply = exchange(replies[k])

time: 407 us -> 359 us (0.88)
  waiting for transfers between devices: 168 us -> 121 us
  Pallas kernels: 57.2 us -> 65 us
  starting transfers between devices: 58.1 us -> 52.8 us
  local copies, waits for them, and re-layouts: 34.8 us -> 30.3 us
    ppermute x3, waiting for transfers between devices: 0.01 us -> 24.2 us  [gather_weight(): lax.ppermute(piece, ('x', 'y'), [(i, i ^ k) for i in range(n_xy)])]
    all_to_all x1 -> x0, waiting for transfers between devices: 23.9 us -> none  [route(): table = lax.all_to_all(table, ALL, split_axis=0, concat_axis=0, tiled=True)]
    all_to_all x8, waiting for transfers between devices: 59.1 us -> 41.8 us  [exchange(): rows = lax.all_to_all(rows, PLANE, split_axis=0, concat_axis=0, tiled=True)]
    ppermute x3, waiting for transfers between devices: 16.4 us -> 0.01 us  [gather_weight(): column.append(lax.ppermute(piece, COLUMN, [(i, i ^ k) for i in range(n_z)]))]
    ppermute x1, waiting for transfers between devices: 16.1 us -> 0.65 us  [step(): text_far = lax.ppermute(text_high, 'zl', SWAP)]
    pallas_call x2 -> x3, Pallas kernels: 52.4 us -> 60.3 us  [answer(): pl.pallas_call(functools.partial(answer_kernel, groups, slots, tb, banks,...]
    unnamed x54 -> x42, local copies, waits for them, and re-layouts: 16.3 us -> 14.7 us
  transfers between devices with their start and end apart: 24 -> 23, of which waited for: 13 -> 13; matrix products, arithmetic and copies ran while one was open for 22% -> 24% of each run, Pallas kernels for 13% -> 17%
where the time goes in v1:
time: 359 us; the launch traced here: 358 us
  waiting for transfers between devices  121 us (34%)
  Pallas kernels  65 us (18%)
  matrix products  54.7 us (15%)
  starting transfers between devices  52.8 us (15%)
  local copies, waits for them, and re-layouts  30.3 us (8%)
  blocking collectives  22.6 us (6%)
  other arithmetic  10 us (3%)
    pallas_call x3, Pallas kernels, answer(): pl.pallas_call(functools.partial(answer_kernel, groups, slots, tb, banks,...  60.3 us
    all_to_all x8, waiting for transfers between devices, exchange(): rows = lax.all_to_all(rows, PLANE, split_axis=0, concat_axis=0, tiled=True)  41.8 us
    all_to_all x8, starting transfers between devices, exchange(): rows = lax.all_to_all(rows, PLANE, split_axis=0, concat_axis=0, tiled=True)  33.6 us
    ppermute x3, waiting for transfers between devices, gather_weight(): lax.ppermute(piece, ('x', 'y'), [(i, i ^ k) for i in range(n_xy)])  24.2 us
    all_to_all x1, blocking collectives, reduce_weight(): lax.all_to_all(total, ('x', 'y'), split_axis=0, concat_axis=0, tiled=True)  22.6 us
    ppermute x1, waiting for transfers between devices, step(): from_low = lax.ppermute(partial[1].astype(bf16), 'zl', SWAP)  21.4 us
    dot_general x1, matrix products, step(): jnp.dot(local_coef, bank, preferred_element_type=f32)  15.5 us
    dot_general x4, matrix products, step(): sent = jnp.dot(pick, texts[k], preferred_element_type=f32).astype(bf16)  15.1 us
  transfers between devices with their start and end apart: 23, of which 13 were waited for; matrix products, arithmetic and copies ran while one was open for 24% of the time, Pallas kernels for 17%

profile of v1, /device:TPU:0, one launch (start us, length us, event | category | flops | bytes accessed | tf_op | source)
XLA Modules:
  0.0 358.1 jit_solution(14664959751174533649)
XLA Ops:
  1.5 0.8 copy.31
  2.5 0.9 convert_element_type.70
  4.1 3.1 collective-permute-start
  7.2 2.6 collective-permute-start.1
  9.8 0.9 collective-permute-start.7
  10.7 3.5 collective-permute-start.9
  15.4 3.8 %convolution_convert_fusion.3 = bf16[768,1152]{1,0:T(8,128)(2,1)} fusion(bf16[512,1152]{1,0:T(8,128)(2,1)} %param.8, s32[768]{0:T(1024)S(1)} %select_n.111), kind=kOutput, calls=%fused_computation.8 | convolution fusion | flops 907247616 | bytes 2952192 | tf_op jit(solution)/shard_map/dot_general | solution.py:326
  19.2 4.3 %all-to-all-start = ((bf16[8,96,1152]{2,1,0:T(8,128)(2,1)}), bf16[8,96,1152]{2,1,0:T(8,128)(2,1)}, u32[]{:S(2)}, u32[]{:S(2)}) async-start(bf16[8,96,1152]{2,1,0:T(8,128)(2,1)} %bitcast.7), calls=%async_computation | async-start | bytes 3538944 | tf_op jit(solution)/shard_map/all_to_all | solution.py:318
  25.1 1.0 pad_maximum_fusion
  26.1 2.0 collective-permute-start.3
  28.1 1.5 collective-permute-start.4
  30.4 1.6 constant_dynamic-update-slice_fusion.5
  32.0 1.5 constant_dynamic-update-slice_fusion.4
  34.7 18.9 %collective-permute-done.3 = bf16[4,40,1152]{2,1,0:T(8,128)(2,1)} collective-permute-done((bf16[4,40,1152]{2,1,0:T(8,128)(2,1)S(1)}, bf16[4,40,1152]{2,1,0:T(8,128)(2,1)}, u32[]{:S(2)}, u32[]{:S(2)}) %collective-permute-start.3) | collective-permute-done | bytes 368672 | tf_op jit(solution)/shard_map/ppermute | solution.py:254
  53.6 1.8 constant_dynamic-update-slice_fusion.2
  55.3 1.8 constant_dynamic-update-slice_fusion.1
  57.1 5.3 %collective-permute-done.5 = bf16[4,40,1152]{2,1,0:T(8,128)(2,1)} collective-permute-done((bf16[4,40,1152]{2,1,0:T(8,128)(2,1)S(1)}, bf16[4,40,1152]{2,1,0:T(8,128)(2,1)}, u32[]{:S(2)}, u32[]{:S(2)}) %collective-permute-start.5) | collective-permute-done | bytes 368672 | tf_op jit(solution)/shard_map/ppermute | solution.py:254
  62.5 1.8 constant_dynamic-update-slice_fusion
  64.3 3.8 %convolution_convert_fusion.2 = bf16[768,1152]{1,0:T(8,128)(2,1)} fusion(bf16[512,1152]{1,0:T(8,128)(2,1)} %collective-permute-done.7, s32[768]{0:T(1024)S(1)} %select_n.119), kind=kOutput, calls=%fused_computation.7 | convolution fusion | flops 907247616 | bytes 2952192 | tf_op jit(solution)/shard_map/dot_general | solution.py:326
  68.1 4.3 %all-to-all-start.1 = ((bf16[8,96,1152]{2,1,0:T(8,128)(2,1)}), bf16[8,96,1152]{2,1,0:T(8,128)(2,1)}, u32[]{:S(2)}, u32[]{:S(2)}) async-start(bf16[8,96,1152]{2,1,0:T(8,128)(2,1)} %bitcast.60), calls=%async_computation.1 | async-start | bytes 3538944 | tf_op jit(solution)/shard_map/all_to_all | solution.py:318
  73.5 3.8 %convolution_convert_fusion.1 = bf16[768,1152]{1,0:T(8,128)(2,1)} fusion(bf16[512,1152]{1,0:T(8,128)(2,1)} %collective-permute-done.9, s32[768]{0:T(1024)S(1)} %select_n.121), kind=kOutput, calls=%fused_computation.6 | convolution fusion | flops 907247616 | bytes 2952192 | tf_op jit(solution)/shard_map/dot_general | solution.py:326
  77.3 1.6 constant_dynamic-update-slice_fusion.7
  78.9 2.5 gather_fusion
  81.4 13.2 %all-to-all-done.1 = bf16[8,96,1152]{2,1,0:T(8,128)(2,1)} async-done(((bf16[8,96,1152]{2,1,0:T(8,128)(2,1)}), bf16[8,96,1152]{2,1,0:T(8,128)(2,1)}, u32[]{:S(2)}, u32[]{:S(2)}) %all-to-all-start.1) | async-done | bytes 1769504 | tf_op jit(solution)/shard_map/all_to_all | solution.py:318
  94.6 4.3 %all-to-all-start.4 = ((bf16[8,96,1152]{2,1,0:T(8,128)(2,1)}), bf16[8,96,1152]{2,1,0:T(8,128)(2,1)}, u32[]{:S(2)}, u32[]{:S(2)}) async-start(bf16[8,96,1152]{2,1,0:T(8,128)(2,1)} %bitcast.62), calls=%async_computation.4 | async-start | bytes 3538944 | tf_op jit(solution)/shard_map/all_to_all | solution.py:318
  99.0 2.2 broadcast_select_fusion
  102.2 3.8 %convolution_convert_fusion = bf16[768,1152]{1,0:T(8,128)(2,1)} fusion(bf16[512,1152]{1,0:T(8,128)(2,1)} %collective-permute-done.10, s32[768]{0:T(1024)S(1)} %select_n.123), kind=kOutput, calls=%fused_computation.5 | convolution fusion | flops 907247616 | bytes 2952192 | tf_op jit(solution)/shard_map/dot_general | solution.py:326
  105.9 15.3 %all-to-all-done.4 = bf16[8,96,1152]{2,1,0:T(8,128)(2,1)} async-done(((bf16[8,96,1152]{2,1,0:T(8,128)(2,1)}), bf16[8,96,1152]{2,1,0:T(8,128)(2,1)}, u32[]{:S(2)}, u32[]{:S(2)}) %all-to-all-start.4) | async-done | bytes 1769504 | tf_op jit(solution)/shard_map/all_to_all | solution.py:318
  121.2 4.3 %all-to-all-start.6 = ((bf16[8,96,1152]{2,1,0:T(8,128)(2,1)}), bf16[8,96,1152]{2,1,0:T(8,128)(2,1)}, u32[]{:S(2)}, u32[]{:S(2)}) async-start(bf16[8,96,1152]{2,1,0:T(8,128)(2,1)} %bitcast.64), calls=%async_computation.6 | async-start | bytes 3538944 | tf_op jit(solution)/shard_map/all_to_all | solution.py:318
  127.0 2.2 reshape.498.refs_2_.refs_1_
  129.2 26.2 %answer.3 = (bf16[768,1152]{1,0:T(8,128)(2,1)}, bf16[768,1152]{1,0:T(8,128)(2,1)}) custom-call(s32[96]{0:T(128)} %reshape.503.tags_ref, bf16[768,1152]{1,0:T(8,128)(2,1)} %bitcast.8.refs_0_, bf16[768,1152]{1,0:T(8,128)(2,1)} %bitcast.10.refs_1_, bf16[1152,1152]{1,0:T(8,128)(2,1)} %reshape.498.refs_2_.refs_1_, bf16[3072,1152]{1,0:T(8,128)(2,1)} %refs_2_.3), custom_call_target="tpu_custom_call" | custom-call | flops 7700742144 | bytes 16809984 | tf_op jit(solution)/shard_map/answer/pallas_call | solution.py:132
  155.4 3.9 %all-to-all-start.3 = ((bf16[8,96,1152]{2,1,0:T(8,128)(2,1)}), bf16[8,96,1152]{2,1,0:T(8,128)(2,1)S(1)}, u32[]{:S(2)}, u32[]{:S(2)}) async-start(bf16[8,96,1152]{2,1,0:T(8,128)(2,1)} %bitcast.66), calls=%async_computation.3 | async-start | bytes 3538944 | tf_op jit(solution)/shard_map/all_to_all | solution.py:318
  160.0 17.4 %answer.5 = bf16[768,1152]{1,0:T(8,128)(2,1)} custom-call(s32[48]{0:T(128)} %squeeze.7.tags_ref, bf16[768,1152]{1,0:T(8,128)(2,1)} %bitcast.20.refs_0_, bf16[1152,1152]{1,0:T(8,128)(2,1)} %reshape.498.refs_2_.refs_1_, bf16[3072,1152]{1,0:T(8,128)(2,1)} %refs_2_.3), custom_call_target="tpu_custom_call" | custom-call | flops 3850371072 | bytes 13271040 | tf_op jit(solution)/shard_map/answer/pallas_call | solution.py:132
  177.4 4.1 %all-to-all-done.3 = bf16[8,96,1152]{2,1,0:T(8,128)(2,1)S(1)} async-done(((bf16[8,96,1152]{2,1,0:T(8,128)(2,1)}), bf16[8,96,1152]{2,1,0:T(8,128)(2,1)S(1)}, u32[]{:S(2)}, u32[]{:S(2)}) %all-to-all-start.3) | async-done | bytes 1769504 | tf_op jit(solution)/shard_map/all_to_all | solution.py:318
  181.5 1.2 copy-done.4
  182.8 3.6 %all-to-all-start.7 = ((bf16[8,96,1152]{2,1,0:T(8,128)(2,1)}), bf16[8,96,1152]{2,1,0:T(8,128)(2,1)S(1)}, u32[]{:S(2)}, u32[]{:S(2)}) async-start(bf16[8,96,1152]{2,1,0:T(8,128)(2,1)} %bitcast.67), calls=%async_computation.7 | async-start | bytes 3538944 | tf_op jit(solution)/shard_map/all_to_all | solution.py:318
  186.4 1.6 copy.47
  188.6 16.7 %answer.4 = bf16[768,1152]{1,0:T(8,128)(2,1)} custom-call(s32[48]{0:T(128)} %squeeze.6.tags_ref, bf16[768,1152]{1,0:T(8,128)(2,1)} %bitcast.16.refs_0_, bf16[1152,1152]{1,0:T(8,128)(2,1)} %reshape.498.refs_2_.refs_1_, bf16[3072,1152]{1,0:T(8,128)(2,1)} %refs_2_.3), custom_call_target="tpu_custom_call" | custom-call | flops 3850371072 | bytes 13271040 | tf_op jit(solution)/shard_map/answer/pallas_call | solution.py:132
  205.3 3.2 all-to-all-done.7
  208.5 1.2 copy-done.6
  209.8 4.3 %all-to-all-start.5 = ((bf16[8,96,1152]{2,1,0:T(8,128)(2,1)}), bf16[8,96,1152]{2,1,0:T(8,128)(2,1)}, u32[]{:S(2)}, u32[]{:S(2)}) async-start(bf16[8,96,1152]{2,1,0:T(8,128)(2,1)} %bitcast.63), calls=%async_computation.5 | async-start | bytes 3538944 | tf_op jit(solution)/shard_map/all_to_all | solution.py:318
  214.1 4.4 %multiply_reduce_fusion = (f32[512]{0:T(512)}, f32[1152,512]{1,0:T(8,128)S(1)}) fusion(bf16[1152,1152]{1,0:T(8,128)(2,1)} %reshape.498.refs_2_.refs_1_, bf16[512,1152]{1,0:T(8,128)(2,1)} %param.8), kind=kOutput, calls=%fused_computation.17 | convolution fusion | flops 1360133632 | bytes 6195200 | tf_op jit(solution)/shard_map/dot_general | solution.py:340
  218.5 2.0 copy.33
  220.5 4.0 %convolution_convert_fusion.4 = bf16[512,1152]{1,0:T(8,128)(2,1)} fusion(bf16[768,1152]{1,0:T(8,128)(2,1)} %bitcast.65, s32[768]{0:T(1024)S(1)} %copy-done.13), kind=kOutput, calls=%fused_computation.9 | convolution fusion | flops 906952704 | bytes 2952192 | tf_op jit(solution)/shard_map/dot_general | solution.py:335
  224.8 1.2 copy-done.5
  226.0 2.4 convolution_convert_fusion.5
  228.3 2.0 collective-permute-start.8
  230.4 6.0 %all-to-all-done.5 = bf16[8,96,1152]{2,1,0:T(8,128)(2,1)} async-done(((bf16[8,96,1152]{2,1,0:T(8,128)(2,1)}), bf16[8,96,1152]{2,1,0:T(8,128)(2,1)}, u32[]{:S(2)}, u32[]{:S(2)}) %all-to-all-start.5) | async-done | bytes 1769504 | tf_op jit(solution)/shard_map/all_to_all | solution.py:318
  236.3 4.5 %all-to-all-start.2 = ((bf16[8,96,1152]{2,1,0:T(8,128)(2,1)}), bf16[8,96,1152]{2,1,0:T(8,128)(2,1)}, u32[]{:S(2)}, u32[]{:S(2)}) async-start(bf16[8,96,1152]{2,1,0:T(8,128)(2,1)} %bitcast.59), calls=%async_computation.2 | async-start | bytes 3538944 | tf_op jit(solution)/shard_map/all_to_all | solution.py:318
  240.9 12.7 %collective-permute-done.11 = bf16[512,1152]{1,0:T(8,128)(2,1)} collective-permute-done((bf16[512,1152]{1,0:T(8,128)(2,1)}, bf16[512,1152]{1,0:T(8,128)(2,1)}, u32[]{:S(2)}, u32[]{:S(2)}) %collective-permute-start.11) | collective-permute-done | bytes 1179680 | tf_op jit(solution)/shard_map/ppermute | solution.py:337
  253.6 4.2 %add_convert_fusion.1 = bf16[512,1152]{1,0:T(8,128)(2,1)} fusion(bf16[512,1152]{1,0:T(8,128)(2,1)} %collective-permute-done.11, bf16[768,1152]{1,0:T(8,128)(2,1)} %bitcast.18, s32[768]{0:T(1024)S(1)} %select_n.121), kind=kOutput, calls=%fused_computation.14 | convolution fusion | flops 908132352 | bytes 4131840 | tf_op jit(solution)/shard_map/dot_general | solution.py:335
  257.8 15.5 %convolution_multiply_fusion = f32[512,1152]{1,0:T(8,128)} fusion(bf16[3072,1152]{1,0:T(8,128)(2,1)} %refs_2_.3, s32[512]{0:T(512)S(1)} %copy-done.15, f32[512,1152]{1,0:T(8,128)S(1)} %divide_bitcast_fusion.unit_ref), kind=kOutput, calls=%fused_computation.3 | convolution fusion | flops 7266238464 | bytes 11798528 | tf_op jit(solution)/shard_map/dot_general | solution.py:348
  273.4 0.9 copy.48.radius_ref
  274.2 21.4 %collective-permute-done.8 = bf16[512,1152]{1,0:T(8,128)(2,1)} collective-permute-done((bf16[512,1152]{1,0:T(8,128)(2,1)}, bf16[512,1152]{1,0:T(8,128)(2,1)}, u32[]{:S(2)}, u32[]{:S(2)}) %collective-permute-start.8) | collective-permute-done | bytes 1179680 | tf_op jit(solution)/shard_map/ppermute | solution.py:339
  295.6 3.9 %convert_add_fusion.base_ref = f32[512,1152]{1,0:T(8,128)S(1)} fusion(bf16[512,1152]{1,0:T(8,128)(2,1)} %collective-permute-done.8, f32[512,1152]{1,0:T(8,128)} %convolution_multiply_fusion, bf16[768,1152]{1,0:T(8,128)(2,1)} %bitcast.12, s32[768]{0:T(1024)S(1)} %select_n.111), kind=kOutput, calls=%fused_computation.15 | convolution fusion | flops 908132352 | bytes 7670784 | tf_op jit(solution)/shard_map/dot_general | solution.py:335
  299.5 11.6 %collective-permute-done.12.high_ref = bf16[512,1152]{1,0:T(8,128)(2,1)} collective-permute-done((bf16[512,1152]{1,0:T(8,128)(2,1)}, bf16[512,1152]{1,0:T(8,128)(2,1)}, u32[]{:S(2)}, u32[]{:S(2)}) %collective-permute-start.12) | collective-permute-done | bytes 1179680 | tf_op jit(solution)/shard_map/ppermute | solution.py:338
  311.2 4.7 %finish.1 = (bf16[512,1152]{1,0:T(8,128)(2,1)S(1)}, bf16[4,4,40,1152]{3,2,1,0:T(8,128)(2,1)S(1)}, f32[4,4,40,1152]{3,2,1,0:T(8,128)S(1)}) custom-call(s32[1]{0:T(128)} %bitcast.c_ref, f32[512,1152]{1,0:T(8,128)S(1)} %convert_add_fusion.base_ref, bf16[512,1152]{1,0:T(8,128)(2,1)} %collective-permute-done.12.high_ref, ...), custom_call_target="tpu_custom_call" | custom-call | flops 1358954496 | bytes 17399808 | tf_op jit(solution)/shard_map/finish/pallas_call | solution.py:201
  316.0 3.3 collective-permute-done.13
  319.5 22.6 %all_to_all.50 = bf16[4,160,1152]{2,1,0:T(8,128)(2,1)S(1)} all-to-all(bf16[4,160,1152]{2,1,0:T(8,128)(2,1)S(1)} %bitcast.58), channel_id=1, replica_groups=mesh['x'=2,'c'=2,'zh'=2,'zl'=2,'y'=2] {'x','y'}, dimensions={0} | all-to-all | bytes 2949120 | tf_op jit(solution)/shard_map/all_to_all | solution.py:294
  342.2 1.0 reduce_sum.61
  343.2 3.5 all-to-all-start.9
  346.7 4.7 %convolution_convert_fusion.6 = bf16[512,1152]{1,0:T(8,128)(2,1)} fusion(bf16[512,1152]{1,0:T(8,128)(2,1)S(1)} %copy-done.2, bf16[1152,1152]{1,0:T(8,128)(2,1)} %reshape.498.refs_2_.refs_1_), kind=kOutput, calls=%fused_computation.11 | convolution fusion | flops 1359544320 | bytes 5013504 | tf_op jit(solution)/shard_map/dot_general | solution.py:357
  351.4 5.7 %all-to-all-done.9 = bf16[4,40,1152]{2,1,0:T(8,128)(2,1)S(1)} async-done(((bf16[4,40,1152]{2,1,0:T(8,128)(2,1)}), bf16[4,40,1152]{2,1,0:T(8,128)(2,1)S(1)}, u32[]{:S(2)}, u32[]{:S(2)}) %all-to-all-start.9) | async-done | bytes 368672 | tf_op jit(solution)/shard_map/all_to_all | solution.py:296
  357.2 0.9 multiply_subtract_fusion
  (133 shorter events, 12.0 us)
Async XLA Ops:
  4.1 19.7 %collective-permute-start = (bf16[1,40,1152]{2,1,0:T(8,128)(2,1)S(1)}, bf16[1,40,1152]{2,1,0:T(8,128)(2,1)S(1)}, u32[]{:S(2)}, u32[]{:S(2)}) collective-permute-start(bf16[1,40,1152]{2,1,0:T(8,128)(2,1)S(1)} %get-tuple-element.24), channel_id=1, source_target_pairs={{0,2},{2,0},{4,6},{6,4},{1,3},{3,1},{5,7},{7,5},{8,10},{10,8},{12,... | collective-permute-start | bytes 276488 | tf_op jit(solution)/shard_map/ppermute | solution.py:249
  7.2 16.7 %collective-permute-start.1 = (bf16[1,40,1152]{2,1,0:T(8,128)(2,1)S(1)}, bf16[1,40,1152]{2,1,0:T(8,128)(2,1)S(1)}, u32[]{:S(2)}, u32[]{:S(2)}) collective-permute-start(bf16[1,40,1152]{2,1,0:T(8,128)(2,1)S(1)} %get-tuple-element.24), channel_id=1, source_target_pairs={{0,4},{2,6},{4,0},{6,2},{1,5},{3,7},{5,1},{7,3},{8,12},{10,14},{12... | collective-permute-start | bytes 276488 | tf_op jit(solution)/shard_map/ppermute | solution.py:249
  9.8 15.4 %collective-permute-start.2 = (bf16[1,40,1152]{2,1,0:T(8,128)(2,1)S(1)}, bf16[1,40,1152]{2,1,0:T(8,128)(2,1)S(1)}, u32[]{:S(2)}, u32[]{:S(2)}) collective-permute-start(bf16[1,40,1152]{2,1,0:T(8,128)(2,1)S(1)} %get-tuple-element.24), channel_id=1, source_target_pairs={{0,6},{2,4},{4,2},{6,0},{1,7},{3,5},{5,3},{7,1},{8,14},{10,12},{12... | collective-permute-start | bytes 276488 | tf_op jit(solution)/shard_map/ppermute | solution.py:249
  9.8 54.5 %collective-permute-start.7 = (bf16[512,1152]{1,0:T(8,128)(2,1)}, bf16[512,1152]{1,0:T(8,128)(2,1)}, u32[]{:S(2)}, u32[]{:S(2)}) collective-permute-start(bf16[512,1152]{1,0:T(8,128)(2,1)} %param.8), channel_id=1, source_target_pairs={{0,2},{2,0},{1,3},{3,1},{4,6},{6,4},{5,7},{7,5},{8,10},{10,8},{9,1... | collective-permute-start | bytes 3538952 | tf_op jit(solution)/shard_map/ppermute | solution.py:309
  10.7 62.8 %collective-permute-start.9 = (bf16[512,1152]{1,0:T(8,128)(2,1)}, bf16[512,1152]{1,0:T(8,128)(2,1)}, u32[]{:S(2)}, u32[]{:S(2)}) collective-permute-start(bf16[512,1152]{1,0:T(8,128)(2,1)} %param.8), channel_id=1, source_target_pairs={{0,4},{4,0},{1,5},{5,1},{2,6},{6,2},{3,7},{7,3},{8,12},{12,8},{9,1... | collective-permute-start | bytes 3538952 | tf_op jit(solution)/shard_map/ppermute | solution.py:310
  19.2 48.9 %all-to-all-start = ((bf16[8,96,1152]{2,1,0:T(8,128)(2,1)}), bf16[8,96,1152]{2,1,0:T(8,128)(2,1)}, u32[]{:S(2)}, u32[]{:S(2)}) async-start(bf16[8,96,1152]{2,1,0:T(8,128)(2,1)} %bitcast.7), calls=%async_computation | async-start | bytes 3538944 | tf_op jit(solution)/shard_map/all_to_all | solution.py:318
  23.8 0.6 copy-start.9
  24.5 0.6 copy-start.8
  26.1 27.4 %collective-permute-start.3 = (bf16[4,40,1152]{2,1,0:T(8,128)(2,1)S(1)}, bf16[4,40,1152]{2,1,0:T(8,128)(2,1)}, u32[]{:S(2)}, u32[]{:S(2)}) collective-permute-start(bf16[4,40,1152]{2,1,0:T(8,128)(2,1)S(1)} %pad_maximum_fusion), channel_id=1, source_target_pairs={{0,1},{1,0},{16,17},{17,16},{2,3},{3,2},{18,19},{19,18},{4,5},{5,4... | collective-permute-start | bytes 1105928 | tf_op jit(solution)/shard_map/ppermute | solution.py:254
  28.1 27.3 %collective-permute-start.4 = (bf16[4,40,1152]{2,1,0:T(8,128)(2,1)S(1)}, bf16[4,40,1152]{2,1,0:T(8,128)(2,1)}, u32[]{:S(2)}, u32[]{:S(2)}) collective-permute-start(bf16[4,40,1152]{2,1,0:T(8,128)(2,1)S(1)} %pad_maximum_fusion), channel_id=1, source_target_pairs={{0,16},{1,17},{16,0},{17,1},{2,18},{3,19},{18,2},{19,3},{4,20},{5,... | collective-permute-start | bytes 1105928 | tf_op jit(solution)/shard_map/ppermute | solution.py:254
  29.6 32.9 %collective-permute-start.5 = (bf16[4,40,1152]{2,1,0:T(8,128)(2,1)S(1)}, bf16[4,40,1152]{2,1,0:T(8,128)(2,1)}, u32[]{:S(2)}, u32[]{:S(2)}) collective-permute-start(bf16[4,40,1152]{2,1,0:T(8,128)(2,1)S(1)} %pad_maximum_fusion), channel_id=1, source_target_pairs={{0,17},{1,16},{16,1},{17,0},{2,19},{3,18},{18,3},{19,2},{4,21},{5,... | collective-permute-start | bytes 1105928 | tf_op jit(solution)/shard_map/ppermute | solution.py:254
  64.3 13.0 %collective-permute-start.6 = (bf16[16,40,1152]{2,1,0:T(8,128)(2,1)}, bf16[16,40,1152]{2,1,0:T(8,128)(2,1)}, u32[]{:S(2)}, u32[]{:S(2)}) collective-permute-start(bf16[16,40,1152]{2,1,0:T(8,128)(2,1)} %get-tuple-element.25), channel_id=1, source_target_pairs={{0,8},{8,0},{1,9},{9,1},{2,10},{10,2},{3,11},{11,3},{4,12},{12,4},... | collective-permute-start | bytes 4423688 | tf_op jit(solution)/shard_map/ppermute | solution.py:256
  68.1 26.6 %all-to-all-start.1 = ((bf16[8,96,1152]{2,1,0:T(8,128)(2,1)}), bf16[8,96,1152]{2,1,0:T(8,128)(2,1)}, u32[]{:S(2)}, u32[]{:S(2)}) async-start(bf16[8,96,1152]{2,1,0:T(8,128)(2,1)} %bitcast.60), calls=%async_computation.1 | async-start | bytes 3538944 | tf_op jit(solution)/shard_map/all_to_all | solution.py:318
  72.9 29.2 %copy-start.12 = (s32[768]{0:T(1024)}, s32[768]{0:T(1024)S(1)}, u32[]{:S(2)}) copy-start(s32[768]{0:T(1024)S(1)} %select_n.123) | copy-start | bytes 9220
  73.4 28.7 %collective-permute-start.10 = (bf16[512,1152]{1,0:T(8,128)(2,1)}, bf16[512,1152]{1,0:T(8,128)(2,1)}, u32[]{:S(2)}, u32[]{:S(2)}) collective-permute-start(bf16[512,1152]{1,0:T(8,128)(2,1)} %collective-permute-done.9), channel_id=1, source_target_pairs={{0,2},{2,0},{1,3},{3,1},{4,6},{6,4},{5,7},{7,5},{8,10},{10,8},{9,1... | collective-permute-start | bytes 3538952 | tf_op jit(solution)/shard_map/ppermute | solution.py:311
  94.6 26.6 %all-to-all-start.4 = ((bf16[8,96,1152]{2,1,0:T(8,128)(2,1)}), bf16[8,96,1152]{2,1,0:T(8,128)(2,1)}, u32[]{:S(2)}, u32[]{:S(2)}) async-start(bf16[8,96,1152]{2,1,0:T(8,128)(2,1)} %bitcast.62), calls=%async_computation.4 | async-start | bytes 3538944 | tf_op jit(solution)/shard_map/all_to_all | solution.py:318
  121.2 34.2 %all-to-all-start.6 = ((bf16[8,96,1152]{2,1,0:T(8,128)(2,1)}), bf16[8,96,1152]{2,1,0:T(8,128)(2,1)}, u32[]{:S(2)}, u32[]{:S(2)}) async-start(bf16[8,96,1152]{2,1,0:T(8,128)(2,1)} %bitcast.64), calls=%async_computation.6 | async-start | bytes 3538944 | tf_op jit(solution)/shard_map/all_to_all | solution.py:318
  155.4 26.1 %all-to-all-start.3 = ((bf16[8,96,1152]{2,1,0:T(8,128)(2,1)}), bf16[8,96,1152]{2,1,0:T(8,128)(2,1)S(1)}, u32[]{:S(2)}, u32[]{:S(2)}) async-start(bf16[8,96,1152]{2,1,0:T(8,128)(2,1)} %bitcast.66), calls=%async_computation.3 | async-start | bytes 3538944 | tf_op jit(solution)/shard_map/all_to_all | solution.py:318
  181.5 1.2 copy-start.4
  182.8 25.8 %all-to-all-start.7 = ((bf16[8,96,1152]{2,1,0:T(8,128)(2,1)}), bf16[8,96,1152]{2,1,0:T(8,128)(2,1)S(1)}, u32[]{:S(2)}, u32[]{:S(2)}) async-start(bf16[8,96,1152]{2,1,0:T(8,128)(2,1)} %bitcast.67), calls=%async_computation.7 | async-start | bytes 3538944 | tf_op jit(solution)/shard_map/all_to_all | solution.py:318
  208.5 1.2 copy-start.6
  209.8 26.6 %all-to-all-start.5 = ((bf16[8,96,1152]{2,1,0:T(8,128)(2,1)}), bf16[8,96,1152]{2,1,0:T(8,128)(2,1)}, u32[]{:S(2)}, u32[]{:S(2)}) async-start(bf16[8,96,1152]{2,1,0:T(8,128)(2,1)} %bitcast.63), calls=%async_computation.5 | async-start | bytes 3538944 | tf_op jit(solution)/shard_map/all_to_all | solution.py:318
  218.5 2.0 copy-start.13
  220.5 4.0 %copy-start.14 = (f32[512]{0:T(512)S(1)}, f32[512]{0:T(512)}, u32[]{:S(2)}) copy-start(f32[512]{0:T(512)} %get-tuple-element.47) | copy-start | bytes 6148
  220.5 4.0 %copy-start.3 = (f32[1152,512]{0,1:T(8,128)S(1)}, f32[1152,512]{0,1:T(8,128)}, u32[]{:S(2)}) copy-start(f32[1152,512]{0,1:T(8,128)} %copy.33) | copy-start | bytes 7077892
  224.5 29.2 %collective-permute-start.11 = (bf16[512,1152]{1,0:T(8,128)(2,1)}, bf16[512,1152]{1,0:T(8,128)(2,1)}, u32[]{:S(2)}, u32[]{:S(2)}) collective-permute-start(bf16[512,1152]{1,0:T(8,128)(2,1)} %convolution_convert_fusion.4), channel_id=1, source_target_pairs={{0,2},{2,0},{1,3},{3,1},{4,6},{6,4},{5,7},{7,5},{8,10},{10,8},{9,1... | collective-permute-start | bytes 3538952 | tf_op jit(solution)/shard_map/ppermute | solution.py:337
  224.5 1.5 copy-start.5
  228.3 67.3 %collective-permute-start.8 = (bf16[512,1152]{1,0:T(8,128)(2,1)}, bf16[512,1152]{1,0:T(8,128)(2,1)}, u32[]{:S(2)}, u32[]{:S(2)}) collective-permute-start(bf16[512,1152]{1,0:T(8,128)(2,1)} %convolution_convert_fusion.5), channel_id=1, source_target_pairs={{0,2},{2,0},{1,3},{3,1},{4,6},{6,4},{5,7},{7,5},{8,10},{10,8},{9,1... | collective-permute-start | bytes 3538952 | tf_op jit(solution)/shard_map/ppermute | solution.py:339
  236.3 37.9 %all-to-all-start.2 = ((bf16[8,96,1152]{2,1,0:T(8,128)(2,1)}), bf16[8,96,1152]{2,1,0:T(8,128)(2,1)}, u32[]{:S(2)}, u32[]{:S(2)}) async-start(bf16[8,96,1152]{2,1,0:T(8,128)(2,1)} %bitcast.59), calls=%async_computation.2 | async-start | bytes 3538944 | tf_op jit(solution)/shard_map/all_to_all | solution.py:318
  253.6 4.2 %copy-start.15 = (s32[512]{0:T(512)S(1)}, s32[512]{0:T(512)}, u32[]{:S(2)}) copy-start(s32[512]{0:T(512)} %param.14) | copy-start | bytes 6148
  257.8 53.4 %collective-permute-start.12 = (bf16[512,1152]{1,0:T(8,128)(2,1)}, bf16[512,1152]{1,0:T(8,128)(2,1)}, u32[]{:S(2)}, u32[]{:S(2)}) collective-permute-start(bf16[512,1152]{1,0:T(8,128)(2,1)} %add_convert_fusion.1), channel_id=1, source_target_pairs={{0,4},{4,0},{1,5},{5,1},{2,6},{6,2},{3,7},{7,3},{8,12},{12,8},{9,1... | collective-permute-start | bytes 3538952 | tf_op jit(solution)/shard_map/ppermute | solution.py:338
  295.6 15.6 %copy-start = (f32[512,1]{1,0:T(8,128)S(1)}, f32[512,1]{1,0:T(8,128)}, u32[]{:S(2)}) copy-start(f32[512,1]{1,0:T(8,128)} %copy.48.radius_ref) | copy-start | bytes 6148
  315.9 3.6 %copy-start.1 = (bf16[512,1152]{1,0:T(8,128)(2,1)}, bf16[512,1152]{1,0:T(8,128)(2,1)S(1)}, u32[]{:S(2)}) copy-start(bf16[512,1152]{1,0:T(8,128)(2,1)S(1)} %get-tuple-element.17) | copy-start | bytes 3538948
  315.9 3.3 collective-permute-start.13
  342.2 4.5 %copy-start.2 = (bf16[512,1152]{1,0:T(8,128)(2,1)S(1)}, bf16[512,1152]{1,0:T(8,128)(2,1)}, u32[]{:S(2)}) copy-start(bf16[512,1152]{1,0:T(8,128)(2,1)} %copy-done.1) | copy-start | bytes 3538948
  343.2 13.9 %all-to-all-start.9 = ((bf16[4,40,1152]{2,1,0:T(8,128)(2,1)}), bf16[4,40,1152]{2,1,0:T(8,128)(2,1)S(1)}, u32[]{:S(2)}, u32[]{:S(2)}) async-start(bf16[4,40,1152]{2,1,0:T(8,128)(2,1)} %bitcast.25), calls=%async_computation.9 | async-start | bytes 737280 | tf_op jit(solution)/shard_map/all_to_all | solution.py:296
  346.7 10.5 %copy-start.7 = (f32[36,1152]{1,0:T(8,128)S(1)}, f32[36,1152]{1,0:T(8,128)}, u32[]{:S(2)}) copy-start(f32[36,1152]{1,0:T(8,128)} %param.9) | copy-start | bytes 497668
  346.7 10.5 %copy-start.10 = (f32[36,1152]{1,0:T(8,128)S(1)}, f32[36,1152]{1,0:T(8,128)}, u32[]{:S(2)}) copy-start(f32[36,1152]{1,0:T(8,128)} %param.10) | copy-start | bytes 497668
  346.7 10.5 %copy-start.11 = (f32[36,1152]{1,0:T(8,128)S(1)}, f32[36,1152]{1,0:T(8,128)}, u32[]{:S(2)}) copy-start(f32[36,1152]{1,0:T(8,128)} %param.11) | copy-start | bytes 497668
